TPU v7x, 32 devices: a whole 2x2x4 slice. The times are simulated.
32 devices in a mesh: band: 4 (over z), head: 4 (over y, x), dp: 2 (over core).
Axes of the slice: x: 2, y: 2, z: 4, core: 2. Of those that a mesh axis runs over, the one named last changes fastest.
Arguments:
- tokens: bfloat16 [32, 1024, 512], P(('dp', 'band'), None, 'head'), parts along dimension 0, may hold values from -6 to 6
- corner_row: int32 [2048], P('dp'), parts along dimension 0, may hold values from 0 to 14
- corner_col: int32 [2048], P('dp'), parts along dimension 0, may hold values from 0 to 1022
- fraction: float32 [2, 2048], P(None, 'dp'), parts along dimension 1, may hold values from 0 to 1
- w_query: bfloat16 [512, 512], P(None, 'head'), may hold values from -2 to 2
- w_key: bfloat16 [512, 512], P(None, 'head'), may hold values from -2 to 2
- w_value: bfloat16 [512, 512], P(None, 'head'), may hold values from -0.25 to 0.25
- w_out: bfloat16 [512, 512], P('head'), may hold values from -0.25 to 0.25
- conv_kernel: float32 [25, 512], P(None, 'head'), may hold values from -1.25 to 1.25
- norm_gain: float32 [512], replicated, may hold values from 0.1 to 1.9
Outputs:
- mixed: bfloat16 [32, 1024, 512], P(('dp', 'band'), None, 'head'), parts along dimension 0
There are 2 independent parts, one for each index of `dp`. A program takes and returns all parts, laid end to end along the dimension named above; an argument that names none is the same for every part. Nothing has to cross between parts.
All inputs are finite; a program needn't handle non-finite values.
Results may differ from a plain program's by a relative error of at most 0.029.
Values may be sent and summed in bfloat16 or wider, within the bound.
A program may use at most 64 MiB of HBM per device.

v0:
```python
import jax
import jax.numpy as jnp
from jax import lax
from jax.sharding import PartitionSpec as P

HEADS = 16
KER = 5


def padded_2(block, sides, width):
    for axis, dim in sides:
        count = lax.axis_size(axis)
        forward = [(i, i + 1) for i in range(count - 1)]
        backward = [(target, source) for source, target in forward]
        low = lax.ppermute(
            lax.slice_in_dim(block, block.shape[dim] - width, None, axis=dim), axis, forward
        )
        high = lax.ppermute(lax.slice_in_dim(block, 0, width, axis=dim), axis, backward)
        block = jnp.concatenate([low, block, high], axis=dim)
    return block


def layer_norm(values, norm_gain):
    values = values.astype(jnp.float32)
    center = jnp.mean(values, axis=-1, keepdims=True)
    spread = jnp.mean(jnp.square(values - center), axis=-1, keepdims=True)
    return ((values - center) * lax.rsqrt(spread + 1e-05) * norm_gain).astype(jnp.bfloat16)


def sample_points(normed, col_table, row_table, count):

    def add_row(index, total):
        plane = lax.dynamic_index_in_dim(normed, index, 0, keepdims=False)
        inner = jnp.dot(col_table, plane, preferred_element_type=jnp.float32)
        weight = lax.dynamic_index_in_dim(row_table, index, 1, keepdims=True)
        return total + weight * inner

    empty = jnp.zeros((count, normed.shape[2]), jnp.float32)
    return lax.fori_loop(0, normed.shape[0], add_row, empty)


def attend(query, key, value, heads):
    count, width = query.shape
    size = width // heads
    block = min(512, count)
    blocks = query.reshape(count // block, block, heads, size)
    key_heads = key.reshape(-1, heads, size)
    value_heads = value.reshape(-1, heads, size)
    scale = 1.0 / size**0.5

    def one_block(part):
        scores = (
            jnp.einsum("qhd,khd->hqk", part, key_heads, preferred_element_type=jnp.float32) * scale
        )
        top = jnp.max(scores, axis=-1, keepdims=True)
        expo = jnp.exp(scores - top)
        probs = (expo / jnp.sum(expo, axis=-1, keepdims=True)).astype(jnp.bfloat16)
        out = jnp.einsum("hqk,khd->qhd", probs, value_heads, preferred_element_type=jnp.float32)
        return out.astype(jnp.bfloat16).reshape(block, width)

    return lax.map(one_block, blocks).reshape(count, width)


def shards(
    tokens, corner_row, corner_col, fraction, w_query, w_key, w_value, w_out, conv_kernel, norm_gain
):
    band_rows, columns, channels = tokens.shape
    whole = lax.all_gather(tokens, "head", axis=2, tiled=True)
    normed = layer_norm(whole, norm_gain)
    width = normed.shape[2]
    count = band_rows * columns
    query = jnp.dot(
        normed.reshape(count, width), w_query, preferred_element_type=jnp.float32
    ).astype(jnp.bfloat16)
    channel_start = lax.axis_index("head") * channels
    normed_here = lax.dynamic_slice_in_dim(normed, channel_start, channels, 2)
    row_top = (1.0 - fraction[0]).astype(jnp.bfloat16)
    row_bottom = fraction[0].astype(jnp.bfloat16)
    col_left = (1.0 - fraction[1]).astype(jnp.bfloat16)
    col_right = fraction[1].astype(jnp.bfloat16)
    positions = lax.broadcasted_iota(jnp.int32, (1, columns), 1)
    zero_bf = jnp.zeros((), jnp.bfloat16)
    col_table = jnp.where(positions == corner_col[:, None], col_left[:, None], zero_bf) + jnp.where(
        positions == corner_col[:, None] + 1, col_right[:, None], zero_bf
    )
    band_start = lax.axis_index("band") * band_rows
    grid_rows = band_start + lax.broadcasted_iota(jnp.int32, (1, band_rows), 1)
    zero_f = jnp.zeros((), jnp.float32)
    row_table = jnp.where(
        grid_rows == corner_row[:, None], row_top.astype(jnp.float32)[:, None], zero_f
    ) + jnp.where(
        grid_rows == corner_row[:, None] + 1, row_bottom.astype(jnp.float32)[:, None], zero_f
    )
    points = corner_row.shape[0]
    share_rows = points // lax.axis_size("band")
    piece = lax.psum_scatter(
        sample_points(normed_here, col_table, row_table, share_rows * lax.axis_size("band")).astype(
            jnp.bfloat16
        ),
        "band",
        scatter_dimension=0,
        tiled=True,
    )
    share = lax.all_gather(piece, "head", axis=1, tiled=True)
    key_share = jnp.dot(share, w_key, preferred_element_type=jnp.float32).astype(jnp.bfloat16)
    value_share = jnp.dot(share, w_value, preferred_element_type=jnp.float32).astype(jnp.bfloat16)
    key, value = (
        lax.all_gather(key_share, "band", axis=0, tiled=True),
        lax.all_gather(value_share, "band", axis=0, tiled=True),
    )
    heads_here = HEADS // lax.axis_size("head")
    attended = attend(query, key, value, heads_here)
    partial_out = jnp.dot(attended, w_out, preferred_element_type=jnp.float32).reshape(
        band_rows, columns, width
    )
    projected = lax.psum_scatter(
        partial_out.astype(jnp.bfloat16), "head", scatter_dimension=2, tiled=True
    ).astype(jnp.float32)
    margin = KER // 2
    rimmed = padded_2(normed_here, (("band", 0),), margin)
    padded = jnp.pad(rimmed, ((0, 0), (margin, margin), (0, 0))).astype(jnp.float32)
    local = jnp.zeros((band_rows, columns, channels), jnp.float32)
    for first in range(KER):
        for second in range(KER):
            local = (
                local
                + conv_kernel[first * KER + second]
                * padded[first : first + band_rows, second : second + columns]
            )
    total = tokens.astype(jnp.float32) + projected + local
    return total.astype(jnp.bfloat16)


def solution(mesh):
    return jax.shard_map(
        shards,
        mesh=mesh,
        in_specs=(
            P(("dp", "band"), None, "head"),
            P("dp"),
            P("dp"),
            P(None, "dp"),
            P(None, "head"),
            P(None, "head"),
            P(None, "head"),
            P("head", None),
            P(None, "head"),
            P(),
        ),
        out_specs=P(("dp", "band"), None, "head"),
        check_vma=False,
    )
```

profile of v0, /device:TPU:0, one launch (start us, length us, event | category | flops | bytes accessed | tf_op | source)
XLA Modules:
  0.0 302.1 jit_solution(5138590391112813641)
XLA Ops:
  11.0 53.4 %all-gather.2.cloned.1.call-done = bf16[4,1024,512]{2,1,0:T(8,128)(2,1)} async-done(((bf16[4,1024,128]{2,1,0:T(8,128)(2,1)}), bf16[4,1024,512]{2,1,0:T(8,128)(2,1)}) %all-gather.2.cloned.1.call-update) | async-done | bytes 4194320 | tf_op jit(solution)/shard_map/all_gather | solution.py:68
  64.4 3.0 convert_reduce_fusion
  73.7 6.7 %while.25 = (s32[]{:T(128)}, f32[1024,128]{0,1:T(8,128)S(1)}, f32[1024,4]{0,1:T(4,128)S(1)}, bf16[4,1024,128]{2,1,0:T(8,128)(2,1)S(1)}, s32[1024]{0:T(1024)S(1)}...) while((s32[]{:T(128)}, f32[1024,128]{0,1:T(8,128)S(1)}, ...), condition=%wide.region_3.4_spmd.clone, body=%wide.region_2.3_spmd.clone.sunk | while | flops 277217280 | bytes 1335423 | solution.py:39
  81.2 3.4 %convolution_convert_fusion = bf16[4096,128]{1,0:T(8,128)(2,1)S(1)} fusion(bf16[4096,512]{1,0:T(8,128)(2,1)} %bitcast.130, bf16[512,128]{1,0:T(8,128)(2,1)S(1)} %copy-done.4), kind=kOutput, calls=%fused_computation.50 | convolution fusion | flops 537395200 | bytes 5373952 | tf_op jit(solution)/shard_map/dot_general | solution.py:72
  85.9 15.3 %reduce-scatter.5.cloned.1.call-done = bf16[256,128]{0,1:T(8,128)(2,1)} async-done(((bf16[1024,128]{0,1:T(8,128)(2,1)}), bf16[256,128]{0,1:T(8,128)(2,1)}) %reduce-scatter.5.cloned.1.call-update) | async-done | bytes 65552 | tf_op jit(solution)/shard_map/reduce_scatter | solution.py:96
  101.3 9.2 %all_gather.13 = bf16[256,512]{0,1:T(8,128)(2,1)S(1)} all-gather(bf16[256,128]{0,1:T(8,128)(2,1)} %reduce-scatter.5.cloned.1.call-done), channel_id=1, replica_groups=mesh['band'=4,'head'=4,'dp'=2] {'head'}, dimensions={1}, use_global_device_ids=true | all-gather | bytes 327680 | tf_op jit(solution)/shard_map/all_gather | solution.py:104
  111.0 14.3 %all_gather.14 = bf16[1024,128]{1,0:T(8,128)(2,1)S(1)} all-gather(bf16[256,128]{1,0:T(8,128)(2,1)S(1)} %convolution_convert_fusion.3), channel_id=1, replica_groups=mesh['band'=4,'head'=4,'dp'=2] {'band'}, dimensions={0}, use_global_device_ids=true | all-gather | bytes 327680 | tf_op jit(solution)/shard_map/all_gather | solution.py:108
  125.5 14.0 %all_gather.15 = bf16[1024,128]{1,0:T(8,128)(2,1)S(1)} all-gather(bf16[256,128]{1,0:T(8,128)(2,1)S(1)} %convolution_convert_fusion.2), channel_id=1, replica_groups=mesh['band'=4,'head'=4,'dp'=2] {'band'}, dimensions={0}, use_global_device_ids=true | all-gather | bytes 327680 | tf_op jit(solution)/shard_map/all_gather | solution.py:109
  139.7 54.7 %while.24 = (s32[]{:T(128)}, bf16[8,512,128]{2,1,0:T(8,128)(2,1)}, bf16[8,512,4,32]{1,3,2,0:T(8,128)(2,1)S(1)}, bf16[1024,4,32]{0,2,1:T(8,128)(2,1)S(1)}, bf16[1024,4,32]{0,2,1:T(8,128)(2,1)S(1)}, /*index=5*/s32[]{:T(128)}) while((s32[]{:T(128)}, bf16[8,512,128]{2,1,0:T(8,128)(2,1)}, bf16[8,512,4,32]{1,3,2,0:T(8,128)(2,1)S(1)}, ...), condition=%wide.region_8.9_spmd, body=%wide.region_5.8_spmd.sunk | while | flops 417402880 | bytes 1720409 | solution.py:61
  139.7 2.9 fusion.147
  142.6 3.1 %fusion.148 = bf16[4,512,32]{1,2,0:T(8,128)(2,1)S(1)} fusion(bf16[1024,4,32]{0,2,1:T(8,128)(2,1)S(1)} %get-tuple-element.358, f32[4,512]{1,0:T(4,128)S(1)} %fusion.147, bf16[1024,4,32]{0,2,1:T(8,128)(2,1)S(1)} %get-tuple-element.357, bf16[8,512,4,32]{1,3,2,0:T(8,128)(2,1)S(1)} %get-tuple-element.356, s32[]{:T(128)S(6)} %copy.42), kind=kOutput, calls=%fused_computation.8.clone.1 | convolution fusion | flops 276892672 | bytes 794628 | tf_op jit(solution)/shard_map/while/body/eval_jaxpr/hqk,khd->qhd/dot_general | solution.py:58
  146.5 2.9 fusion.147
  149.5 3.1 %fusion.148 = bf16[4,512,32]{1,2,0:T(8,128)(2,1)S(1)} fusion(bf16[1024,4,32]{0,2,1:T(8,128)(2,1)S(1)} %get-tuple-element.358, f32[4,512]{1,0:T(4,128)S(1)} %fusion.147, bf16[1024,4,32]{0,2,1:T(8,128)(2,1)S(1)} %get-tuple-element.357, bf16[8,512,4,32]{1,3,2,0:T(8,128)(2,1)S(1)} %get-tuple-element.356, s32[]{:T(128)S(6)} %copy.42), kind=kOutput, calls=%fused_computation.8.clone.1 | convolution fusion | flops 276892672 | bytes 794628 | tf_op jit(solution)/shard_map/while/body/eval_jaxpr/hqk,khd->qhd/dot_general | solution.py:58
  153.4 2.9 fusion.147
  156.3 3.1 %fusion.148 = bf16[4,512,32]{1,2,0:T(8,128)(2,1)S(1)} fusion(bf16[1024,4,32]{0,2,1:T(8,128)(2,1)S(1)} %get-tuple-element.358, f32[4,512]{1,0:T(4,128)S(1)} %fusion.147, bf16[1024,4,32]{0,2,1:T(8,128)(2,1)S(1)} %get-tuple-element.357, bf16[8,512,4,32]{1,3,2,0:T(8,128)(2,1)S(1)} %get-tuple-element.356, s32[]{:T(128)S(6)} %copy.42), kind=kOutput, calls=%fused_computation.8.clone.1 | convolution fusion | flops 276892672 | bytes 794628 | tf_op jit(solution)/shard_map/while/body/eval_jaxpr/hqk,khd->qhd/dot_general | solution.py:58
  160.2 2.9 fusion.147
  163.1 3.1 %fusion.148 = bf16[4,512,32]{1,2,0:T(8,128)(2,1)S(1)} fusion(bf16[1024,4,32]{0,2,1:T(8,128)(2,1)S(1)} %get-tuple-element.358, f32[4,512]{1,0:T(4,128)S(1)} %fusion.147, bf16[1024,4,32]{0,2,1:T(8,128)(2,1)S(1)} %get-tuple-element.357, bf16[8,512,4,32]{1,3,2,0:T(8,128)(2,1)S(1)} %get-tuple-element.356, s32[]{:T(128)S(6)} %copy.42), kind=kOutput, calls=%fused_computation.8.clone.1 | convolution fusion | flops 276892672 | bytes 794628 | tf_op jit(solution)/shard_map/while/body/eval_jaxpr/hqk,khd->qhd/dot_general | solution.py:58
  167.0 2.9 fusion.147
  170.0 3.1 %fusion.148 = bf16[4,512,32]{1,2,0:T(8,128)(2,1)S(1)} fusion(bf16[1024,4,32]{0,2,1:T(8,128)(2,1)S(1)} %get-tuple-element.358, f32[4,512]{1,0:T(4,128)S(1)} %fusion.147, bf16[1024,4,32]{0,2,1:T(8,128)(2,1)S(1)} %get-tuple-element.357, bf16[8,512,4,32]{1,3,2,0:T(8,128)(2,1)S(1)} %get-tuple-element.356, s32[]{:T(128)S(6)} %copy.42), kind=kOutput, calls=%fused_computation.8.clone.1 | convolution fusion | flops 276892672 | bytes 794628 | tf_op jit(solution)/shard_map/while/body/eval_jaxpr/hqk,khd->qhd/dot_general | solution.py:58
  173.8 2.9 fusion.147
  176.8 3.1 %fusion.148 = bf16[4,512,32]{1,2,0:T(8,128)(2,1)S(1)} fusion(bf16[1024,4,32]{0,2,1:T(8,128)(2,1)S(1)} %get-tuple-element.358, f32[4,512]{1,0:T(4,128)S(1)} %fusion.147, bf16[1024,4,32]{0,2,1:T(8,128)(2,1)S(1)} %get-tuple-element.357, bf16[8,512,4,32]{1,3,2,0:T(8,128)(2,1)S(1)} %get-tuple-element.356, s32[]{:T(128)S(6)} %copy.42), kind=kOutput, calls=%fused_computation.8.clone.1 | convolution fusion | flops 276892672 | bytes 794628 | tf_op jit(solution)/shard_map/while/body/eval_jaxpr/hqk,khd->qhd/dot_general | solution.py:58
  180.7 2.9 fusion.147
  183.6 3.1 %fusion.148 = bf16[4,512,32]{1,2,0:T(8,128)(2,1)S(1)} fusion(bf16[1024,4,32]{0,2,1:T(8,128)(2,1)S(1)} %get-tuple-element.358, f32[4,512]{1,0:T(4,128)S(1)} %fusion.147, bf16[1024,4,32]{0,2,1:T(8,128)(2,1)S(1)} %get-tuple-element.357, bf16[8,512,4,32]{1,3,2,0:T(8,128)(2,1)S(1)} %get-tuple-element.356, s32[]{:T(128)S(6)} %copy.42), kind=kOutput, calls=%fused_computation.8.clone.1 | convolution fusion | flops 276892672 | bytes 794628 | tf_op jit(solution)/shard_map/while/body/eval_jaxpr/hqk,khd->qhd/dot_general | solution.py:58
  187.5 2.9 fusion.147
  190.4 3.1 %fusion.148 = bf16[4,512,32]{1,2,0:T(8,128)(2,1)S(1)} fusion(bf16[1024,4,32]{0,2,1:T(8,128)(2,1)S(1)} %get-tuple-element.358, f32[4,512]{1,0:T(4,128)S(1)} %fusion.147, bf16[1024,4,32]{0,2,1:T(8,128)(2,1)S(1)} %get-tuple-element.357, bf16[8,512,4,32]{1,3,2,0:T(8,128)(2,1)S(1)} %get-tuple-element.356, s32[]{:T(128)S(6)} %copy.42), kind=kOutput, calls=%fused_computation.8.clone.1 | convolution fusion | flops 276892672 | bytes 794628 | tf_op jit(solution)/shard_map/while/body/eval_jaxpr/hqk,khd->qhd/dot_general | solution.py:58
  194.3 4.4 %convolution_convert_fusion.1 = bf16[4,1024,512]{2,1,0:T(8,128)(2,1)} fusion(bf16[4,1024,128]{2,1,0:T(8,128)(2,1)} %bitcast.137, bf16[128,512]{1,0:T(8,128)(2,1)S(1)} %copy-done), kind=kOutput, calls=%fused_computation.52 | convolution fusion | flops 538968064 | bytes 5373952 | tf_op jit(solution)/shard_map/dot_general | solution.py:113
  198.8 8.1 %copy.24 = bf16[4,1024,512]{1,0,2:T(4,128)(2,1)} copy(bf16[4,1024,512]{2,1,0:T(8,128)(2,1)} %convolution_convert_fusion.1) | data formatting | bytes 8388608
  206.9 6.4 %copy.30 = bf16[64,8,4,1024]{3,1,2,0:T(8,128)(2,1)} copy(bf16[64,8,4,1024]{3,2,1,0:T(4,128)(2,1)} %bitcast.132) | data formatting | bytes 8388608
  217.6 5.1 %collective-permute-done = bf16[2,1024,128]{2,1,0:T(8,128)(2,1)S(1)} collective-permute-done((bf16[2,1024,128]{2,1,0:T(8,128)(2,1)S(1)}, bf16[2,1024,128]{2,1,0:T(8,128)(2,1)S(1)}, u32[]{:S(2)}, u32[]{:S(2)}) %collective-permute-start) | collective-permute-done | bytes 524320 | tf_op jit(solution)/shard_map/ppermute | solution.py:15
  222.7 4.4 %collective-permute-done.1 = bf16[2,1024,128]{2,1,0:T(8,128)(2,1)S(1)} collective-permute-done((bf16[2,1024,128]{2,1,0:T(8,128)(2,1)S(1)}, bf16[2,1024,128]{2,1,0:T(8,128)(2,1)S(1)}, u32[]{:S(2)}, u32[]{:S(2)}) %collective-permute-start.1) | collective-permute-done | bytes 524320 | tf_op jit(solution)/shard_map/ppermute | solution.py:18
  229.5 34.2 %reduce-scatter.7.cloned.1.call-done = bf16[128,4096]{1,0:T(8,128)(2,1)} async-done(((bf16[512,4096]{1,0:T(8,128)(2,1)}), bf16[128,4096]{1,0:T(8,128)(2,1)}) %reduce-scatter.7.cloned.1.call-update) | async-done | bytes 1048592
  266.5 29.1 %fusion.88 = bf16[4,1024,128]{2,1,0:T(8,128)(2,1)} fusion(f32[8,1028,128]{2,1,0:T(8,128)} %fusion.85, bf16[4,1024,128]{2,1,0:T(8,128)(2,1)S(1)} %copy.25, bf16[4,1024,128]{2,1,0:T(8,128)(2,1)S(1)} %copy-done.3, f32[128]{0:T(128)S(1)} %get-tuple-element.229, f32[128]{0:T(128)S(1)} %get-tuple-element.230, f32[128]{0:T(128)S(1)} %get-tuple-element.207, ...), kind=kLoop, calls=%fused_computation.62 | loop fusion | flops 28311552 | bytes 55587328 | tf_op jit(solution)/shard_map/convert_element_type | solution.py:131
  (79 shorter events, 35.9 us)
Async XLA Ops:
  6.5 187.8 %copy-start = (bf16[128,512]{1,0:T(8,128)(2,1)S(1)}, bf16[128,512]{1,0:T(8,128)(2,1)}, u32[]{:S(2)}) copy-start(bf16[128,512]{1,0:T(8,128)(2,1)} %param.21) | copy-start | bytes 393220
  6.5 57.8 %all-gather.2.cloned.1.call-start = ((), (), s32[]{:S(2)}) async-start(), calls=%async_computation.2 | async-start | bytes 5242880 | tf_op jit(solution)/shard_map/all_gather | solution.py:68
  7.3 94.0 %reduce-scatter.5.cloned.1.call-start = ((), (), s32[]{:S(2)}) async-start(), calls=%async_computation.3 | async-start | bytes 327680 | tf_op jit(solution)/shard_map/reduce_scatter | solution.py:96
  64.4 3.4 %copy-start.1 = (bf16[4,1024,512]{2,1,0:T(8,128)(2,1)S(1)}, bf16[4,1024,512]{2,1,0:T(8,128)(2,1)}, u32[]{:S(2)}) copy-start(bf16[4,1024,512]{2,1,0:T(8,128)(2,1)} %all-gather.2.cloned.1.call-done) | copy-start | bytes 12582916
  67.8 1.6 copy-start.9
  71.1 1.9 copy-start.2
  73.0 0.7 copy-start.8
  73.7 7.5 %copy-start.4 = (bf16[512,128]{1,0:T(8,128)(2,1)S(1)}, bf16[512,128]{1,0:T(8,128)(2,1)}, u32[]{:S(2)}) copy-start(bf16[512,128]{1,0:T(8,128)(2,1)} %param.18) | copy-start | bytes 393220
  81.1 182.5 %reduce-scatter.7.cloned.1.call-start = ((), (), s32[]{:S(2)}) async-start(), calls=%async_computation.4 | async-start | bytes 5242880
  85.2 25.3 %copy-start.5 = (bf16[512,128]{1,0:T(8,128)(2,1)S(1)}, bf16[512,128]{1,0:T(8,128)(2,1)}, u32[]{:S(2)}) copy-start(bf16[512,128]{1,0:T(8,128)(2,1)} %param.20) | copy-start | bytes 393220
  85.2 25.6 %copy-start.6 = (bf16[512,128]{1,0:T(8,128)(2,1)S(1)}, bf16[512,128]{1,0:T(8,128)(2,1)}, u32[]{:S(2)}) copy-start(bf16[512,128]{1,0:T(8,128)(2,1)} %param.19) | copy-start | bytes 393220
  213.4 4.2 %copy-start.7 = (f32[25,128]{1,0:T(8,128)S(1)}, f32[25,128]{1,0:T(8,128)}, u32[]{:S(2)}) copy-start(f32[25,128]{1,0:T(8,128)} %param.22) | copy-start | bytes 38404
  214.7 8.0 %collective-permute-start = (bf16[2,1024,128]{2,1,0:T(8,128)(2,1)S(1)}, bf16[2,1024,128]{2,1,0:T(8,128)(2,1)S(1)}, u32[]{:S(2)}, u32[]{:S(2)}) collective-permute-start(bf16[2,1024,128]{2,1,0:T(8,128)(2,1)S(1)} %get-tuple-element.204), channel_id=1, source_target_pairs={{0,8},{8,16},{16,24},{1,9},{9,17},{17,25},{2,10},{10,18},{18,26},{... | collective-permute-start | bytes 1572872 | tf_op jit(solution)/shard_map/ppermute | solution.py:15
  216.0 11.1 %collective-permute-start.1 = (bf16[2,1024,128]{2,1,0:T(8,128)(2,1)S(1)}, bf16[2,1024,128]{2,1,0:T(8,128)(2,1)S(1)}, u32[]{:S(2)}, u32[]{:S(2)}) collective-permute-start(bf16[2,1024,128]{2,1,0:T(8,128)(2,1)S(1)} %get-tuple-element.205), channel_id=1, source_target_pairs={{8,0},{16,8},{24,16},{9,1},{17,9},{25,17},{10,2},{18,10},{26,18},{... | collective-permute-start | bytes 1572872 | tf_op jit(solution)/shard_map/ppermute | solution.py:18
  229.5 37.0 %copy-start.3 = (bf16[4,1024,128]{2,1,0:T(8,128)(2,1)S(1)}, bf16[4,1024,128]{2,1,0:T(8,128)(2,1)}, u32[]{:S(2)}) copy-start(bf16[4,1024,128]{2,1,0:T(8,128)(2,1)} %param.14) | copy-start | bytes 3145732
Sparse Core Ops, SparseCore 0:
  9.2 55.1 all-gather.1
  81.2 19.9 reduce-scatter.4
  213.5 50.1 reduce-scatter.6
where the time goes:
time: 303 us; the launch traced here: 302 us
  waiting for transfers between devices  113 us (37%)
  matrix products  63.1 us (21%)
  other arithmetic  42 us (14%)
  blocking collectives  37.5 us (12%)
  local copies, waits for them, and re-layouts  29.8 us (10%)
  between operations  13.4 us (4%)
    all_gather x1, waiting for transfers between devices, shards(): whole = lax.all_gather(tokens, 'head', axis=2, tiled=True)  53.4 us
    unnamed x4, waiting for transfers between devices  34.9 us
    convert_element_type x1, other arithmetic, shards(): return total.astype(jnp.bfloat16)  29.1 us
    dot_general x8, matrix products, one_block(): jnp.einsum('hqk,khd->qhd', probs, value_heads, preferred_element_type=jnp...  24.7 us
    sub x8, matrix products, one_block(): expo = jnp.exp(scores - top)  23.4 us
    unnamed x25, local copies, waits for them, and re-layouts  20.7 us
    reduce_scatter x1, waiting for transfers between devices, shards(): lax.psum_scatter(sample_points(normed_here, col_table, row_table, share_r...  15.3 us
    all_gather x1, blocking collectives, shards(): lax.all_gather(key_share, 'band', axis=0, tiled=True)  14.3 us
  transfers between devices with their start and end apart: 5, of which 5 were waited for; matrix products, arithmetic and copies ran while one was open for 4% of the time, Pallas kernels for 0%

commit v1 on v0

--- a/solution.py
+++ b/solution.py
@@ -5,6 +5,16 @@
 
 HEADS = 16
 KER = 5
+
+
+def gather_by_hops(x, axis, d):
+    size = lax.axis_size(axis)
+    held, shards = (x, [x])
+    for _ in range(size - 1):
+        held = lax.ppermute(held, axis, [(i, (i + 1) % size) for i in range(size)])
+        shards.insert(0, held)
+    line = jnp.concatenate(shards, axis=d)
+    return jnp.roll(line, (lax.axis_index(axis) + 1) * x.shape[d], axis=d)
 
 
 def padded_2(block, sides, width):
@@ -65,7 +75,7 @@
     tokens, corner_row, corner_col, fraction, w_query, w_key, w_value, w_out, conv_kernel, norm_gain
 ):
     band_rows, columns, channels = tokens.shape
-    whole = lax.all_gather(tokens, "head", axis=2, tiled=True)
+    whole = gather_by_hops(tokens, "head", 2)
     normed = layer_norm(whole, norm_gain)
     width = normed.shape[2]
     count = band_rows * columns

time: 303 us -> 324 us (1.069)
  waiting for transfers between devices: 113 us -> 125 us
  starting transfers between devices: 2.92 us -> 9.89 us
  local copies, waits for them, and re-layouts: 29.8 us -> 34.3 us
    ppermute x0 -> x3, waiting for transfers between devices: none -> 69.5 us  [gather_by_hops(): held = lax.ppermute(held, axis, [(i, (i + 1) % size) for i in range(size)])]
    all_gather x1 -> x0, waiting for transfers between devices: 53.4 us -> none  [shards(): whole = lax.all_gather(tokens, 'head', axis=2, tiled=True)]
    unnamed x25 -> x40, local copies, waits for them, and re-layouts: 20.7 us -> 24.8 us
    ppermute x0 -> x3, starting transfers between devices: none -> 3.76 us  [gather_by_hops(): held = lax.ppermute(held, axis, [(i, (i + 1) % size) for i in range(size)])]
    ppermute x1, waiting for transfers between devices: 5.08 us -> 1.46 us  [padded_2(): lax.ppermute(lax.slice_in_dim(block, block.shape[dim] - width, None, axis...]
    ppermute x1, starting transfers between devices: 1.32 us -> 4.8 us  [padded_2(): lax.ppermute(lax.slice_in_dim(block, block.shape[dim] - width, None, axis...]
    unnamed x4 -> x3, waiting for transfers between devices: 34.9 us -> 34 us
  transfers between devices with their start and end apart: 5 -> 7, of which waited for: 5 -> 7; matrix products, arithmetic and copies ran while one was open for 4% -> 4% of each run, Pallas kernels for 0% -> 0%
where the time goes in v1:
time: 324 us; the launch traced here: 323 us
  waiting for transfers between devices  125 us (39%)
  matrix products  63.1 us (19%)
  other arithmetic  39.6 us (12%)
  blocking collectives  37.5 us (12%)
  local copies, waits for them, and re-layouts  34.3 us (11%)
  between operations  13.7 us (4%)
  starting transfers between devices  9.89 us (3%)
    ppermute x3, waiting for transfers between devices, gather_by_hops(): held = lax.ppermute(held, axis, [(i, (i + 1) % size) for i in range(size)])  69.5 us
    unnamed x3, waiting for transfers between devices  34 us
    convert_element_type x1, other arithmetic, shards(): return total.astype(jnp.bfloat16)  28.7 us
    unnamed x40, local copies, waits for them, and re-layouts  24.8 us
    dot_general x8, matrix products, one_block(): jnp.einsum('hqk,khd->qhd', probs, value_heads, preferred_element_type=jnp...  24.8 us
    sub x8, matrix products, one_block(): expo = jnp.exp(scores - top)  23.5 us
    reduce_scatter x1, waiting for transfers between devices, shards(): lax.psum_scatter(sample_points(normed_here, col_table, row_table, share_r...  15.1 us
    all_gather x1, blocking collectives, shards(): lax.all_gather(key_share, 'band', axis=0, tiled=True)  14.2 us
  transfers between devices with their start and end apart: 7, of which 7 were waited for; matrix products, arithmetic and copies ran while one was open for 4% of the time, Pallas kernels for 0%

profile of v1, /device:TPU:0, one launch (start us, length us, event | category | flops | bytes accessed | tf_op | source)
XLA Modules:
  0.0 323.2 jit_solution(7547039699296865175)
XLA Ops:
  6.5 3.0 collective-permute-start
  9.5 24.3 %collective-permute-done = bf16[4,1024,128]{2,1,0:T(8,128)(2,1)S(1)} collective-permute-done((bf16[4,1024,128]{2,1,0:T(8,128)(2,1)}, bf16[4,1024,128]{2,1,0:T(8,128)(2,1)S(1)}, u32[]{:S(2)}, u32[]{:S(2)}) %collective-permute-start) | collective-permute-done | bytes 1048608 | tf_op jit(solution)/shard_map/ppermute | solution.py:14
  34.6 24.4 %collective-permute-done.1 = bf16[4,1024,128]{2,1,0:T(8,128)(2,1)S(1)} collective-permute-done((bf16[4,1024,128]{2,1,0:T(8,128)(2,1)S(1)}, bf16[4,1024,128]{2,1,0:T(8,128)(2,1)S(1)}, u32[]{:S(2)}, u32[]{:S(2)}) %collective-permute-start.1) | collective-permute-done | bytes 1048608 | tf_op jit(solution)/shard_map/ppermute | solution.py:14
  62.7 20.7 %collective-permute-done.2 = bf16[4,1024,128]{2,1,0:T(8,128)(2,1)S(1)} collective-permute-done((bf16[4,1024,128]{2,1,0:T(8,128)(2,1)S(1)}, bf16[4,1024,128]{2,1,0:T(8,128)(2,1)S(1)}, u32[]{:S(2)}, u32[]{:S(2)}) %collective-permute-start.2) | collective-permute-done | bytes 1048608 | tf_op jit(solution)/shard_map/ppermute | solution.py:14
  94.9 6.7 %while.25 = (s32[]{:T(128)}, f32[1024,128]{0,1:T(8,128)S(1)}, f32[1024,4]{0,1:T(4,128)S(1)}, bf16[4,1024,128]{2,1,0:T(8,128)(2,1)S(1)}, s32[1024]{0:T(1024)S(1)}...) while((s32[]{:T(128)}, f32[1024,128]{0,1:T(8,128)S(1)}, ...), condition=%wide.region_3.4_spmd.clone, body=%wide.region_2.3_spmd.clone.sunk | while | flops 277217280 | bytes 1335423 | solution.py:49
  102.7 3.4 %convolution_convert_fusion = bf16[4096,128]{1,0:T(8,128)(2,1)S(1)} fusion(bf16[4096,512]{1,0:T(8,128)(2,1)} %bitcast.130, bf16[512,128]{1,0:T(8,128)(2,1)S(1)} %copy-done.8), kind=kOutput, calls=%fused_computation.50 | convolution fusion | flops 537395200 | bytes 5373952 | tf_op jit(solution)/shard_map/dot_general | solution.py:82
  107.4 15.1 %reduce-scatter.5.cloned.1.call-done = bf16[256,128]{0,1:T(8,128)(2,1)} async-done(((bf16[1024,128]{0,1:T(8,128)(2,1)}), bf16[256,128]{0,1:T(8,128)(2,1)}) %reduce-scatter.5.cloned.1.call-update) | async-done | bytes 65552 | tf_op jit(solution)/shard_map/reduce_scatter | solution.py:106
  122.5 9.2 %all_gather.9 = bf16[256,512]{0,1:T(8,128)(2,1)S(1)} all-gather(bf16[256,128]{0,1:T(8,128)(2,1)} %reduce-scatter.5.cloned.1.call-done), channel_id=1, replica_groups=mesh['band'=4,'head'=4,'dp'=2] {'head'}, dimensions={1}, use_global_device_ids=true | all-gather | bytes 327680 | tf_op jit(solution)/shard_map/all_gather | solution.py:114
  132.0 14.2 %all_gather.10 = bf16[1024,128]{1,0:T(8,128)(2,1)S(1)} all-gather(bf16[256,128]{1,0:T(8,128)(2,1)S(1)} %convolution_convert_fusion.3), channel_id=1, replica_groups=mesh['band'=4,'head'=4,'dp'=2] {'band'}, dimensions={0}, use_global_device_ids=true | all-gather | bytes 327680 | tf_op jit(solution)/shard_map/all_gather | solution.py:118
  146.7 14.0 %all_gather.11 = bf16[1024,128]{1,0:T(8,128)(2,1)S(1)} all-gather(bf16[256,128]{1,0:T(8,128)(2,1)S(1)} %convolution_convert_fusion.2), channel_id=1, replica_groups=mesh['band'=4,'head'=4,'dp'=2] {'band'}, dimensions={0}, use_global_device_ids=true | all-gather | bytes 327680 | tf_op jit(solution)/shard_map/all_gather | solution.py:119
  160.9 54.7 %while.24 = (s32[]{:T(128)}, bf16[8,512,128]{2,1,0:T(8,128)(2,1)}, bf16[8,512,4,32]{1,3,2,0:T(8,128)(2,1)S(1)}, bf16[1024,4,32]{0,2,1:T(8,128)(2,1)S(1)}, bf16[1024,4,32]{0,2,1:T(8,128)(2,1)S(1)}, /*index=5*/s32[]{:T(128)}) while((s32[]{:T(128)}, bf16[8,512,128]{2,1,0:T(8,128)(2,1)}, bf16[8,512,4,32]{1,3,2,0:T(8,128)(2,1)S(1)}, ...), condition=%wide.region_8.9_spmd, body=%wide.region_5.8_spmd.sunk | while | flops 417402880 | bytes 1720409 | solution.py:71
  160.9 2.9 fusion.147
  163.8 3.1 fusion.148
  167.7 2.9 fusion.147
  170.6 3.1 fusion.148
  174.5 2.9 fusion.147
  177.5 3.1 fusion.148
  181.4 2.9 fusion.147
  184.3 3.1 fusion.148
  188.2 2.9 fusion.147
  191.2 3.1 fusion.148
  198.0 3.1 fusion.148
  204.8 3.1 fusion.148
  208.7 2.9 fusion.147
  211.7 3.1 fusion.148
  215.6 4.4 %convolution_convert_fusion.1 = bf16[4,1024,512]{2,1,0:T(8,128)(2,1)} fusion(bf16[4,1024,128]{2,1,0:T(8,128)(2,1)} %bitcast.137, bf16[128,512]{1,0:T(8,128)(2,1)S(1)} %copy-done), kind=kOutput, calls=%fused_computation.52 | convolution fusion | flops 538968064 | bytes 5373952 | tf_op jit(solution)/shard_map/dot_general | solution.py:123
  220.0 8.1 %copy.24 = bf16[4,1024,512]{1,0,2:T(4,128)(2,1)} copy(bf16[4,1024,512]{2,1,0:T(8,128)(2,1)} %convolution_convert_fusion.1) | data formatting | bytes 8388608
  228.1 6.4 %copy.30 = bf16[64,8,4,1024]{3,1,2,0:T(8,128)(2,1)} copy(bf16[64,8,4,1024]{3,2,1,0:T(4,128)(2,1)} %bitcast.132) | data formatting | bytes 8388608
  237.3 4.8 %collective-permute-start.3 = (bf16[2,1024,128]{2,1,0:T(8,128)(2,1)S(1)}, bf16[2,1024,128]{2,1,0:T(8,128)(2,1)S(1)}, u32[]{:S(2)}, u32[]{:S(2)}) collective-permute-start(bf16[2,1024,128]{2,1,0:T(8,128)(2,1)S(1)} %get-tuple-element.204), channel_id=1, source_target_pairs={{0,8},{8,16},{16,24},{1,9},{9,17},{17,25},{2,10},{10,18},{18,26},{... | collective-permute-start | bytes 1572872 | tf_op jit(solution)/shard_map/ppermute | solution.py:25
  242.1 4.9 %collective-permute-done.4 = bf16[2,1024,128]{2,1,0:T(8,128)(2,1)S(1)} collective-permute-done((bf16[2,1024,128]{2,1,0:T(8,128)(2,1)S(1)}, bf16[2,1024,128]{2,1,0:T(8,128)(2,1)S(1)}, u32[]{:S(2)}, u32[]{:S(2)}) %collective-permute-start.4) | collective-permute-done | bytes 524320 | tf_op jit(solution)/shard_map/ppermute | solution.py:28
  250.9 33.9 %reduce-scatter.7.cloned.1.call-done = bf16[128,4096]{1,0:T(8,128)(2,1)} async-done(((bf16[512,4096]{1,0:T(8,128)(2,1)}), bf16[128,4096]{1,0:T(8,128)(2,1)}) %reduce-scatter.7.cloned.1.call-update) | async-done | bytes 1048592
  287.7 28.7 %fusion.88 = bf16[4,1024,128]{2,1,0:T(8,128)(2,1)} fusion(f32[8,1028,128]{2,1,0:T(8,128)} %fusion.85, bf16[4,1024,128]{2,1,0:T(8,128)(2,1)S(1)} %copy.25, bf16[4,1024,128]{2,1,0:T(8,128)(2,1)S(1)} %copy-done.2, f32[128]{0:T(128)S(1)} %get-tuple-element.229, f32[128]{0:T(128)S(1)} %get-tuple-element.230, f32[128]{0:T(128)S(1)} %get-tuple-element.207, ...), kind=kLoop, calls=%fused_computation.62 | loop fusion | flops 28311552 | bytes 55587328 | tf_op jit(solution)/shard_map/convert_element_type | solution.py:141
  (98 shorter events, 47.1 us)
Async XLA Ops:
  6.5 209.0 %copy-start = (bf16[128,512]{1,0:T(8,128)(2,1)S(1)}, bf16[128,512]{1,0:T(8,128)(2,1)}, u32[]{:S(2)}) copy-start(bf16[128,512]{1,0:T(8,128)(2,1)} %param.21) | copy-start | bytes 393220
  6.5 116.0 %reduce-scatter.5.cloned.1.call-start = ((), (), s32[]{:S(2)}) async-start(), calls=%async_computation.2 | async-start | bytes 327680 | tf_op jit(solution)/shard_map/reduce_scatter | solution.py:106
  6.5 27.3 %collective-permute-start = (bf16[4,1024,128]{2,1,0:T(8,128)(2,1)}, bf16[4,1024,128]{2,1,0:T(8,128)(2,1)S(1)}, u32[]{:S(2)}, u32[]{:S(2)}) collective-permute-start(bf16[4,1024,128]{2,1,0:T(8,128)(2,1)} %param.14), channel_id=1, source_target_pairs={{0,2},{2,4},{4,6},{6,0},{1,3},{3,5},{5,7},{7,1},{8,10},{10,12},{12... | collective-permute-start | bytes 3145736 | tf_op jit(solution)/shard_map/ppermute | solution.py:14
  33.8 25.2 %collective-permute-start.1 = (bf16[4,1024,128]{2,1,0:T(8,128)(2,1)S(1)}, bf16[4,1024,128]{2,1,0:T(8,128)(2,1)S(1)}, u32[]{:S(2)}, u32[]{:S(2)}) collective-permute-start(bf16[4,1024,128]{2,1,0:T(8,128)(2,1)S(1)} %collective-permute-done), channel_id=1, source_target_pairs={{0,2},{2,4},{4,6},{6,0},{1,3},{3,5},{5,7},{7,1},{8,10},{10,12},{12... | collective-permute-start | bytes 3145736 | tf_op jit(solution)/shard_map/ppermute | solution.py:14
  59.1 24.4 %collective-permute-start.2 = (bf16[4,1024,128]{2,1,0:T(8,128)(2,1)S(1)}, bf16[4,1024,128]{2,1,0:T(8,128)(2,1)S(1)}, u32[]{:S(2)}, u32[]{:S(2)}) collective-permute-start(bf16[4,1024,128]{2,1,0:T(8,128)(2,1)S(1)} %collective-permute-done.1), channel_id=1, source_target_pairs={{0,2},{2,4},{4,6},{6,0},{1,3},{3,5},{5,7},{7,1},{8,10},{10,12},{12... | collective-permute-start | bytes 3145736 | tf_op jit(solution)/shard_map/ppermute | solution.py:14
  83.4 1.0 copy-start.3
  84.7 1.2 copy-start.2
  85.1 1.3 copy-start.4
  88.5 1.8 copy-start.13
  91.9 1.9 copy-start.1
  93.9 1.0 copy-start.7
  93.9 1.0 copy-start.12
  94.9 7.7 %copy-start.8 = (bf16[512,128]{1,0:T(8,128)(2,1)S(1)}, bf16[512,128]{1,0:T(8,128)(2,1)}, u32[]{:S(2)}) copy-start(bf16[512,128]{1,0:T(8,128)(2,1)} %param.18) | copy-start | bytes 393220
  101.6 1.1 copy-start.5
  102.4 182.4 %reduce-scatter.7.cloned.1.call-start = ((), (), s32[]{:S(2)}) async-start(), calls=%async_computation.3 | async-start | bytes 5242880
  106.6 25.1 %copy-start.9 = (bf16[512,128]{1,0:T(8,128)(2,1)S(1)}, bf16[512,128]{1,0:T(8,128)(2,1)}, u32[]{:S(2)}) copy-start(bf16[512,128]{1,0:T(8,128)(2,1)} %param.19) | copy-start | bytes 393220
  107.1 39.3 %copy-start.10 = (bf16[512,128]{1,0:T(8,128)(2,1)S(1)}, bf16[512,128]{1,0:T(8,128)(2,1)}, u32[]{:S(2)}) copy-start(bf16[512,128]{1,0:T(8,128)(2,1)} %param.20) | copy-start | bytes 393220
  234.5 7.5 %copy-start.11 = (f32[25,128]{1,0:T(8,128)S(1)}, f32[25,128]{1,0:T(8,128)}, u32[]{:S(2)}) copy-start(f32[25,128]{1,0:T(8,128)} %param.22) | copy-start | bytes 38404
  234.6 13.9 %copy-start.6 = (bf16[4,1024,128]{2,1,0:T(8,128)(2,1)S(1)}, bf16[4,1024,128]{2,1,0:T(8,128)(2,1)}, u32[]{:S(2)}) copy-start(bf16[4,1024,128]{2,1,0:T(8,128)(2,1)} %copy-done.5) | copy-start | bytes 3145732
  236.0 11.1 %collective-permute-start.4 = (bf16[2,1024,128]{2,1,0:T(8,128)(2,1)S(1)}, bf16[2,1024,128]{2,1,0:T(8,128)(2,1)S(1)}, u32[]{:S(2)}, u32[]{:S(2)}) collective-permute-start(bf16[2,1024,128]{2,1,0:T(8,128)(2,1)S(1)} %get-tuple-element.205), channel_id=1, source_target_pairs={{8,0},{16,8},{24,16},{9,1},{17,9},{25,17},{10,2},{18,10},{26,18},{... | collective-permute-start | bytes 1572872 | tf_op jit(solution)/shard_map/ppermute | solution.py:28
  237.3 11.2 %collective-permute-start.3 = (bf16[2,1024,128]{2,1,0:T(8,128)(2,1)S(1)}, bf16[2,1024,128]{2,1,0:T(8,128)(2,1)S(1)}, u32[]{:S(2)}, u32[]{:S(2)}) collective-permute-start(bf16[2,1024,128]{2,1,0:T(8,128)(2,1)S(1)} %get-tuple-element.204), channel_id=1, source_target_pairs={{0,8},{8,16},{16,24},{1,9},{9,17},{17,25},{2,10},{10,18},{18,26},{... | collective-permute-start | bytes 1572872 | tf_op jit(solution)/shard_map/ppermute | solution.py:25
Sparse Core Ops, SparseCore 0:
  102.6 19.9 reduce-scatter.4
  234.7 50.1 reduce-scatter.6
